TPU v7x, 32 devices: a whole 2x2x4 slice. The times are simulated.
32 devices in a mesh: dp: 8 (over z, y), tensor: 4 (over x, core).
Axes of the slice: x: 2, y: 2, z: 4, core: 2. Of those that a mesh axis runs over, the one named last changes fastest.
Arguments:
- gradients: bfloat16 [8, 2, 256, 1792], P('dp', None, None, 'tensor'), may hold values from -16 to 16, as said below
- errors: float32 [8, 2, 256, 1792], P('dp', None, None, 'tensor'), may hold values from -4 to 4
- start_factors: float32 [2, 1792, 32], P(None, 'tensor'), may hold values from -5 to 5
- moments: float32 [2, 256, 1792], P(None, 'dp', 'tensor'), may hold values from -2 to 2
- weights: float32 [2, 256, 1792], P(None, 'dp', 'tensor'), may hold values from -5 to 5
- vector_grads: bfloat16 [8, 5, 1792], P('dp', None, 'tensor'), may hold values from -16 to 16, as said below
- vector_moments: float32 [5, 1792], P(None, 'tensor'), may hold values from -2 to 2
- vector_weights: float32 [5, 1792], P(None, 'tensor'), may hold values from 0.5 to 1.5
Outputs:
- new_errors: float32 [8, 2, 256, 1792], P('dp', None, None, 'tensor')
- new_moments: float32 [2, 256, 1792], P(None, 'dp', 'tensor')
- new_weights: bfloat16 [2, 256, 1792], P(None, None, 'tensor')
- new_vector_moments: float32 [5, 1792], P(None, 'tensor')
- new_vector_weights: float32 [5, 1792], P(None, 'tensor')
Inputs may be any that keep to these rules, and one draw needn't show every extreme that they name: `gradients`: each replica's gradient is a part common to all replicas plus its own part. `vector_grads`: each replica's gradient is a part common to all replicas plus its own part.
All inputs are finite; a program needn't handle non-finite values.
Results may differ from a plain program's by a relative error of at most 0.0004.
Values may be sent and summed in bfloat16 or wider, within the bound.
A program may use at most 64 MiB of HBM per device.

v0:
```python
import jax
import jax.numpy as jnp
from jax import lax
from jax.sharding import PartitionSpec as P

ROUNDS = 2
momentum_coef = 0.9
step_rate = 0.1


def basis_from(gram_mat, summed):
    factor_low = jnp.linalg.cholesky(gram_mat)
    return lax.linalg.triangular_solve(
        factor_low, summed, left_side=False, lower=True, transpose_a=True
    )


def left_basis(mixed, right_f):
    partial_value = jnp.einsum("mkd,mdr->mkr", mixed, right_f, precision=lax.Precision.HIGHEST)
    summed = lax.psum(partial_value, ("dp", "tensor"))
    gram_mat = jnp.einsum("mkr,mks->mrs", summed, summed, precision=lax.Precision.HIGHEST)
    return basis_from(gram_mat, summed)


def update(mixed, start, moments, weights):
    right_f = start
    for round_idx in range(ROUNDS):
        basis_now = left_basis(mixed, right_f)
        right_part = jnp.einsum("mkd,mkr->mdr", mixed, basis_now, precision=lax.Precision.HIGHEST)
        right_f = lax.psum(right_part, "dp")
    replicas = lax.axis_size("dp")
    approx = (
        jnp.einsum("mkr,mdr->mkd", basis_now, right_f, precision=lax.Precision.HIGHEST) / replicas
    )
    fresh_errors = mixed - approx
    own_rows = moments.shape[1]
    my_rows = lax.dynamic_slice_in_dim(approx, lax.axis_index("dp") * own_rows, own_rows, 1)
    fresh_moments = momentum_coef * moments + my_rows
    fresh_weights = (weights - step_rate * fresh_moments).astype(jnp.bfloat16)
    regathered = lax.all_gather(fresh_weights, "dp", axis=1, tiled=True)
    return (fresh_errors, fresh_moments, regathered)


def per_device(
    gradients, errors, start_factors, moments, weights, vector_grads, vector_moments, vector_weights
):
    mixed = gradients[0].astype(jnp.float32) + errors[0]
    fresh_errors, fresh_moments, regathered = update(mixed, start_factors, moments, weights)
    vector_total = lax.psum(vector_grads[0].astype(jnp.float32), "dp")
    vector_mean = vector_total / lax.axis_size("dp")
    fresh_vector_moments = momentum_coef * vector_moments + vector_mean
    fresh_vector_weights = vector_weights - step_rate * fresh_vector_moments
    return (
        fresh_errors[None],
        fresh_moments,
        regathered,
        fresh_vector_moments,
        fresh_vector_weights,
    )


def solution(mesh):
    in_specs = (
        P("dp", None, None, "tensor"),
        P("dp", None, None, "tensor"),
        P(None, "tensor", None),
        P(None, "dp", "tensor"),
        P(None, "dp", "tensor"),
        P("dp", None, "tensor"),
        P(None, "tensor"),
        P(None, "tensor"),
    )
    out_specs = (
        P("dp", None, None, "tensor"),
        P(None, "dp", "tensor"),
        P(None, None, "tensor"),
        P(None, "tensor"),
        P(None, "tensor"),
    )
    return jax.shard_map(
        per_device, mesh=mesh, in_specs=in_specs, out_specs=out_specs, check_vma=False
    )
```

profile of v0, /device:TPU:0, one launch (start us, length us, event | category | flops | bytes accessed | tf_op | source)
XLA Modules:
  0.0 471.9 jit_solution(15930844537223940268)
XLA Ops:
  7.2 0.0 copy-start
  7.2 0.0 copy-start.1
  7.2 0.0 all-reduce.5.cloned.1.call-start
  7.2 0.8 copy-done
  8.1 2.6 fusion.6
  10.7 0.0 copy-start.2
  10.7 0.0 all-reduce.5.cloned.1.call-update
  10.7 0.0 all-reduce.7.cloned.1.call-start
  10.8 123.7 %all-reduce.5.cloned.1.call-done = f32[2,256,32]{1,2,0:T(8,128)} async-done(((f32[2,256,32]{1,2,0:T(8,128)}), f32[2,256,32]{1,2,0:T(8,128)}) %all-reduce.5.cloned.1.call-update) | async-done | bytes 65552 | tf_op jit(solution)/shard_map/psum | solution.py:20
  134.5 1.1 fusion.13
  135.6 0.1 copy.27
  135.7 5.9 %custom-call.8 = f32[2,32,32]{2,1,0:T(8,128)S(1)} custom-call(f32[2,32,32]{2,1,0:T(8,128)S(1)} %fusion.12), custom_call_target="Cholesky" | custom-call | tf_op jit(solution)/shard_map/jit(cholesky)/cholesky | solution.py:12
  141.6 0.1 compare_reduce_fusion.1
  141.7 0.1 select_bitcast_fusion.1
  141.8 4.9 %custom-call.9 = f32[2,1,32,32]{2,3,1,0:T(8,128)S(1)} custom-call(f32[2,1,32,32]{3,2,1,0:T(8,128)S(1)} %select_bitcast_fusion.1), custom_call_target="InvertDiagBlocksLowerTriangular" | custom-call | tf_op jit(solution)/shard_map/triangular_solve/custom-call.0 | solution.py:13
  146.7 1.1 convolution_bitcast_fusion.1
  147.8 0.0 copy-done.1
  147.8 0.0 copy-done.2
  147.8 1.6 fusion.4
  149.4 0.0 all-reduce.7.cloned.1.call-update
  149.5 0.0 all-reduce.9.cloned.1.call-start
  149.5 70.5 %all-reduce.7.cloned.1.call-done = f32[2,448,32]{1,2,0:T(8,128)} async-done(((f32[2,448,32]{1,2,0:T(8,128)}), f32[2,448,32]{1,2,0:T(8,128)}) %all-reduce.7.cloned.1.call-update) | async-done | bytes 114704 | tf_op jit(solution)/shard_map/psum | solution.py:30
  220.0 0.0 copy-start.4
  220.0 2.3 fusion.2
  222.3 0.0 copy-start.8
  222.3 0.0 all-reduce.9.cloned.1.call-update
  222.3 0.0 all-reduce.11.cloned.1.call-start
  222.4 0.6 copy-done.8
  223.0 0.0 copy-done.4
  223.0 0.0 copy-start.5
  223.0 0.2 copy.31
  223.2 0.7 copy-done.5
  223.9 0.2 copy.32
  224.1 35.5 %psum.39 = f32[5,448]{1,0:T(8,128)S(1)} all-reduce(f32[5,448]{1,0:T(8,128)S(1)} %bitcast_convert_fusion), channel_id=1, replica_groups=mesh['dp'=8,'tensor'=4] {'dp'}, use_global_device_ids=true, to_apply=%region_6.9 | all-reduce | flops 2240 | bytes 17920 | tf_op jit(solution)/shard_map/psum | solution.py:49
  259.6 84.4 %all-reduce.9.cloned.1.call-done = f32[2,256,32]{1,2,0:T(8,128)} async-done(((f32[2,256,32]{1,2,0:T(8,128)}), f32[2,256,32]{1,2,0:T(8,128)}) %all-reduce.9.cloned.1.call-update) | async-done | bytes 65552 | tf_op jit(solution)/shard_map/psum | solution.py:20
  344.0 1.1 fusion.14
  345.1 0.1 copy.29
  345.1 0.0 copy-start.3
  345.2 5.9 %custom-call.10 = f32[2,32,32]{2,1,0:T(8,128)S(1)} custom-call(f32[2,32,32]{2,1,0:T(8,128)S(1)} %fusion.10), custom_call_target="Cholesky" | custom-call | tf_op jit(solution)/shard_map/jit(cholesky)/cholesky | solution.py:12
  351.1 0.1 compare_reduce_fusion
  351.2 0.1 select_bitcast_fusion
  351.3 4.9 %custom-call.11 = f32[2,1,32,32]{2,3,1,0:T(8,128)S(1)} custom-call(f32[2,1,32,32]{3,2,1,0:T(8,128)S(1)} %select_bitcast_fusion), custom_call_target="InvertDiagBlocksLowerTriangular" | custom-call | tf_op jit(solution)/shard_map/triangular_solve/custom-call.0 | solution.py:13
  356.2 0.0 copy-done.3
  356.2 0.3 convolution_bitcast_fusion
  356.5 1.6 fusion
  358.1 0.0 copy-start.6
  358.1 0.0 copy-start.7
  358.1 0.0 all-reduce.11.cloned.1.call-update
  358.1 0.7 copy-done.6
  358.8 0.0 copy-done.7
  358.8 0.6 multiply_subtract_fusion
  359.4 69.2 %all-reduce.11.cloned.1.call-done = f32[2,448,32]{1,2,0:T(8,128)} async-done(((f32[2,448,32]{1,2,0:T(8,128)}), f32[2,448,32]{1,2,0:T(8,128)}) %all-reduce.11.cloned.1.call-update) | async-done | bytes 114704 | tf_op jit(solution)/shard_map/psum | solution.py:30
  428.7 1.8 convolution_multiply_fusion
  430.5 1.1 fusion.8
  431.6 0.2 subtract_convert_fusion
  431.8 0.1 copy.33
  431.9 0.8 copy.34
  432.8 31.5 %all_gather.3 = bf16[2,256,448]{2,0,1:T(2,128)(2,1)S(1)} all-gather(bf16[2,32,448]{2,0,1:T(2,128)(2,1)S(1)} %copy.33), channel_id=1, replica_groups=mesh['dp'=8,'tensor'=4] {'dp'}, dimensions={1}, use_global_device_ids=true | all-gather | bytes 516096 | tf_op jit(solution)/shard_map/all_gather | solution.py:40
  464.3 1.1 copy.35
  (7 shorter events, 0.1 us)
Async XLA Ops:
  7.2 0.9 copy-start
  7.2 140.6 %copy-start.1 = (f32[1,2,256,448]{2,3,1,0:T(8,128)S(1)}, f32[1,2,256,448]{2,3,1,0:T(8,128)}, u32[]{:S(2)}) copy-start(f32[1,2,256,448]{2,3,1,0:T(8,128)} %param.12) | copy-start | bytes 2752516
  7.2 127.3 %all-reduce.5.cloned.1.call-start = ((), (), s32[]{:S(2)}) async-start(), calls=%async_computation | async-start | bytes 131072 | tf_op jit(solution)/shard_map/psum | solution.py:20
  10.7 137.1 %copy-start.2 = (bf16[1,2,256,448]{2,3,1,0:T(8,128)(2,1)S(1)}, bf16[1,2,256,448]{2,3,1,0:T(8,128)(2,1)}, u32[]{:S(2)}) copy-start(bf16[1,2,256,448]{2,3,1,0:T(8,128)(2,1)} %param.11) | copy-start | bytes 1376260
  10.7 209.3 %all-reduce.7.cloned.1.call-start = ((), (), s32[]{:S(2)}) async-start(), calls=%async_computation.1 | async-start | bytes 262144 | tf_op jit(solution)/shard_map/psum | solution.py:30
  149.5 194.5 %all-reduce.9.cloned.1.call-start = ((), (), s32[]{:S(2)}) async-start(), calls=%async_computation.2 | async-start | bytes 131072 | tf_op jit(solution)/shard_map/psum | solution.py:20
  220.0 3.0 copy-start.4
  222.3 0.7 copy-start.8
  222.3 206.3 %all-reduce.11.cloned.1.call-start = ((), (), s32[]{:S(2)}) async-start(), calls=%async_computation.3 | async-start | bytes 262144 | tf_op jit(solution)/shard_map/psum | solution.py:30
  223.0 0.9 copy-start.5
  345.1 11.0 %copy-start.3 = (f32[2,256,32]{1,2,0:T(8,128)S(1)}, f32[2,256,32]{1,2,0:T(8,128)}, u32[]{:S(2)}) copy-start(f32[2,256,32]{1,2,0:T(8,128)} %all-reduce.9.cloned.1.call-done) | copy-start | bytes 196612
  358.1 0.7 copy-start.6
  358.1 0.7 copy-start.7
Sparse Core Ops, SparseCore 0:
  14.2 120.2 all-reduce.4
  149.6 70.3 all-reduce.6
  227.1 116.7 all-reduce.8
  358.2 70.3 all-reduce.10
where the time goes:
time: 472 us
  waiting for transfers between devices  348 us (74%)
  blocking collectives  67 us (14%)
  other arithmetic  23.9 us (5%)
  between operations  13.9 us (3%)
  matrix products  13.6 us (3%)
  local copies, waits for them, and re-layouts  5.47 us (1%)
    psum x2, waiting for transfers between devices, left_basis(): summed = lax.psum(partial_value, ('dp', 'tensor'))  208 us
    psum x2, waiting for transfers between devices, update(): right_f = lax.psum(right_part, 'dp')  140 us
    psum x1, blocking collectives, per_device(): vector_total = lax.psum(vector_grads[0].astype(jnp.float32), 'dp')  35.5 us
    all_gather x1, blocking collectives, update(): regathered = lax.all_gather(fresh_weights, 'dp', axis=1, tiled=True)  31.5 us
    another operation x7, other arithmetic, basis_from(): factor_low = jnp.linalg.cholesky(gram_mat)  12 us
    another operation x5, other arithmetic, basis_from(): lax.linalg.triangular_solve(factor_low, summed, left_side=False, lower=Tr...  9.99 us
  transfers between devices with their start and end apart: 4, of which 4 were waited for; matrix products, arithmetic and copies ran while one was open for 0% of the time, Pallas kernels for 0%

commit v1 on v0

--- a/solution.py
+++ b/solution.py
@@ -37,7 +37,22 @@
     my_rows = lax.dynamic_slice_in_dim(approx, lax.axis_index("dp") * own_rows, own_rows, 1)
     fresh_moments = momentum_coef * moments + my_rows
     fresh_weights = (weights - step_rate * fresh_moments).astype(jnp.bfloat16)
-    regathered = lax.all_gather(fresh_weights, "dp", axis=1, tiled=True)
+    ways, here, step = (lax.axis_size("dp"), lax.axis_index("dp"), fresh_weights.shape[1])
+    shape = [n * ways if d == 1 else n for d, n in enumerate(fresh_weights.shape)]
+    regathered = lax.dynamic_update_slice_in_dim(
+        jnp.zeros(shape, fresh_weights.dtype), fresh_weights, here * step, axis=1
+    )
+    going_up = going_down = fresh_weights
+    for far in range(1, ways // 2 + 1):
+        going_up = lax.ppermute(going_up, "dp", [(d, (d + 1) % ways) for d in range(ways)])
+        regathered = lax.dynamic_update_slice_in_dim(
+            regathered, going_up, (here - far) % ways * step, axis=1
+        )
+        if 2 * far < ways:
+            going_down = lax.ppermute(going_down, "dp", [(d, (d - 1) % ways) for d in range(ways)])
+            regathered = lax.dynamic_update_slice_in_dim(
+                regathered, going_down, (here + far) % ways * step, axis=1
+            )
     return (fresh_errors, fresh_moments, regathered)
 
 

time: 472 us -> 518 us (1.097)
  waiting for transfers between devices: 348 us -> 396 us
  blocking collectives: 67 us -> 35.3 us
  local copies, waits for them, and re-layouts: 5.47 us -> 22 us
  starting transfers between devices: 0.16 us -> 11.5 us
    psum x2, waiting for transfers between devices: 208 us -> 245 us  [left_basis(): summed = lax.psum(partial_value, ('dp', 'tensor'))]
    all_gather x1 -> x0, blocking collectives: 31.5 us -> none  [update(): regathered = lax.all_gather(fresh_weights, 'dp', axis=1, tiled=True)]
    dynamic_update_slice x0 -> x8, local copies, waits for them, and re-layouts: none -> 16.6 us  [the longest x4 7.88 us: update(): lax.dynamic_update_slice_in_dim(regathered, going_up, (here - far) % ways...]
    ppermute x0 -> x7, waiting for transfers between devices: none -> 12.6 us  [the longest x3 6.92 us: update(): lax.ppermute(going_down, 'dp', [(d, (d - 1) % ways) for d in range(ways)])]
    ppermute x0 -> x7, starting transfers between devices: none -> 11.3 us  [the longest x4 7.34 us: update(): lax.ppermute(going_up, 'dp', [(d, (d + 1) % ways) for d in range(ways)])]
  transfers between devices with their start and end apart: 4 -> 11, of which waited for: 4 -> 6; matrix products, arithmetic and copies ran while one was open for 0% -> 4% of each run, Pallas kernels for 0% -> 0%
where the time goes in v1:
time: 518 us; the launch traced here: 517 us
  waiting for transfers between devices  396 us (76%)
  blocking collectives  35.3 us (7%)
  other arithmetic  24.6 us (5%)
  local copies, waits for them, and re-layouts  22 us (4%)
  between operations  14 us (3%)
  matrix products  13.6 us (3%)
  starting transfers between devices  11.5 us (2%)
    psum x2, waiting for transfers between devices, left_basis(): summed = lax.psum(partial_value, ('dp', 'tensor'))  245 us
    psum x2, waiting for transfers between devices, update(): right_f = lax.psum(right_part, 'dp')  138 us
    psum x1, blocking collectives, per_device(): vector_total = lax.psum(vector_grads[0].astype(jnp.float32), 'dp')  35.3 us
    another operation x7, other arithmetic, basis_from(): factor_low = jnp.linalg.cholesky(gram_mat)  12 us
  transfers between devices with their start and end apart: 11, of which 6 were waited for; matrix products, arithmetic and copies ran while one was open for 4% of the time, Pallas kernels for 0%

profile of v1, /device:TPU:0, one launch (start us, length us, event | category | flops | bytes accessed | tf_op | source)
XLA Modules:
  0.0 517.3 jit_solution(17698577803345100730)
XLA Ops:
  7.2 0.0 copy-start
  7.2 0.0 all-reduce.5.cloned.1.call-start
  7.2 0.8 copy-done
  8.1 2.6 fusion.6
  10.7 0.0 all-reduce.5.cloned.1.call-update
  10.7 0.0 all-reduce.7.cloned.1.call-start
  10.8 123.6 %all-reduce.5.cloned.1.call-done = f32[2,256,32]{1,2,0:T(8,128)} async-done(((f32[2,256,32]{1,2,0:T(8,128)}), f32[2,256,32]{1,2,0:T(8,128)}) %all-reduce.5.cloned.1.call-update) | async-done | bytes 65552 | tf_op jit(solution)/shard_map/psum | solution.py:20
  134.5 1.1 fusion.13
  135.6 0.1 copy.19
  135.7 5.9 %custom-call.8 = f32[2,32,32]{2,1,0:T(8,128)S(1)} custom-call(f32[2,32,32]{2,1,0:T(8,128)S(1)} %fusion.12), custom_call_target="Cholesky" | custom-call | tf_op jit(solution)/shard_map/jit(cholesky)/cholesky | solution.py:12
  141.5 0.1 compare_reduce_fusion.1
  141.7 0.1 select_bitcast_fusion.1
  141.7 4.9 custom-call.9
  146.7 1.1 convolution_bitcast_fusion.1
  147.8 1.6 fusion.4
  149.4 0.0 all-reduce.7.cloned.1.call-update
  149.5 0.0 all-reduce.9.cloned.1.call-start
  149.5 70.5 %all-reduce.7.cloned.1.call-done = f32[2,448,32]{1,2,0:T(8,128)} async-done(((f32[2,448,32]{1,2,0:T(8,128)}), f32[2,448,32]{1,2,0:T(8,128)}) %all-reduce.7.cloned.1.call-update) | async-done | bytes 114704 | tf_op jit(solution)/shard_map/psum | solution.py:30
  220.0 2.2 fusion.2
  222.3 0.0 all-reduce.9.cloned.1.call-update
  222.3 0.0 all-reduce.11.cloned.1.call-start
  222.3 121.6 %all-reduce.9.cloned.1.call-done = f32[2,256,32]{1,2,0:T(8,128)} async-done(((f32[2,256,32]{1,2,0:T(8,128)}), f32[2,256,32]{1,2,0:T(8,128)}) %all-reduce.9.cloned.1.call-update) | async-done | bytes 65552 | tf_op jit(solution)/shard_map/psum | solution.py:20
  344.0 1.1 fusion.14
  345.1 0.1 copy.20
  345.2 5.9 %custom-call.10 = f32[2,32,32]{2,1,0:T(8,128)S(1)} custom-call(f32[2,32,32]{2,1,0:T(8,128)S(1)} %fusion.10), custom_call_target="Cholesky" | custom-call | tf_op jit(solution)/shard_map/jit(cholesky)/cholesky | solution.py:12
  351.1 0.1 compare_reduce_fusion
  351.2 0.1 select_bitcast_fusion
  351.3 4.9 custom-call.11
  356.2 0.3 convolution_bitcast_fusion
  356.5 1.6 fusion
  358.1 0.0 all-reduce.11.cloned.1.call-update
  358.1 0.9 copy-done.6
  359.0 0.2 copy.22
  359.2 0.7 copy-done.7
  359.9 1.0 copy.23
  360.9 67.8 %all-reduce.11.cloned.1.call-done = f32[2,448,32]{1,2,0:T(8,128)} async-done(((f32[2,448,32]{1,2,0:T(8,128)}), f32[2,448,32]{1,2,0:T(8,128)}) %all-reduce.11.cloned.1.call-update) | async-done | bytes 114704 | tf_op jit(solution)/shard_map/psum | solution.py:30
  428.7 1.9 convolution_multiply_fusion
  430.6 0.0 copy-start.10
  430.6 0.9 subtract_convert_fusion
  431.5 0.8 collective-permute-start
  432.3 3.9 collective-permute-start.1
  436.2 5.7 %collective-permute-done = bf16[2,32,448]{1,2,0:T(8,128)(2,1)S(1)} collective-permute-done((bf16[2,32,448]{1,2,0:T(8,128)(2,1)}, bf16[2,32,448]{1,2,0:T(8,128)(2,1)S(1)}, u32[]{:S(2)}, u32[]{:S(2)}) %collective-permute-start) | collective-permute-done | bytes 57376 | tf_op jit(solution)/shard_map/ppermute | solution.py:47
  441.9 2.5 collective-permute-start.2
  444.4 0.0 copy-start.9
  444.4 35.3 %psum.39 = f32[5,448]{1,0:T(8,128)S(1)} all-reduce(f32[5,448]{1,0:T(8,128)S(1)} %bitcast_convert_fusion), channel_id=1, replica_groups=mesh['dp'=8,'tensor'=4] {'dp'}, use_global_device_ids=true, to_apply=%region_6.9 | all-reduce | flops 2240 | bytes 17920 | tf_op jit(solution)/shard_map/psum | solution.py:64
  479.7 0.0 collective-permute-done.1
  479.7 0.0 collective-permute-start.3
  479.7 2.0 collective-permute-start.4
  481.8 0.6 multiply_subtract_fusion
  482.4 6.9 %collective-permute-done.3 = bf16[2,32,448]{1,2,0:T(8,128)(2,1)} collective-permute-done((bf16[2,32,448]{1,2,0:T(8,128)(2,1)S(1)}, bf16[2,32,448]{1,2,0:T(8,128)(2,1)}, u32[]{:S(2)}, u32[]{:S(2)}) %collective-permute-start.3) | collective-permute-done | bytes 57376 | tf_op jit(solution)/shard_map/ppermute | solution.py:52
  489.3 0.0 collective-permute-start.5
  489.3 2.0 collective-permute-start.6
  491.3 1.1 fusion.8
  492.4 1.8 dynamic_update_slice.24
  494.2 0.8 copy.24
  495.1 1.6 dynamic_update_slice.25
  496.6 1.9 dynamic_update_slice.26
  498.5 2.4 dynamic_update_slice.27
  500.9 2.5 dynamic_update_slice.28
  503.4 2.4 dynamic_update_slice.29
  505.8 2.5 dynamic_update_slice.30
  508.4 1.6 dynamic_update_slice.31
  510.0 0.0 copy-start.5
  510.0 0.8 copy-done.5
  (26 shorter events, 0.2 us)
Async XLA Ops:
  7.2 0.9 copy-start
  7.2 140.6 %copy-start.1 = (f32[1,2,256,448]{2,3,1,0:T(8,128)S(1)}, f32[1,2,256,448]{2,3,1,0:T(8,128)}, u32[]{:S(2)}) copy-start(f32[1,2,256,448]{2,3,1,0:T(8,128)} %param.12) | copy-start | bytes 2752516
  7.2 127.3 %all-reduce.5.cloned.1.call-start = ((), (), s32[]{:S(2)}) async-start(), calls=%async_computation | async-start | bytes 131072 | tf_op jit(solution)/shard_map/psum | solution.py:20
  10.7 137.1 %copy-start.2 = (bf16[1,2,256,448]{2,3,1,0:T(8,128)(2,1)S(1)}, bf16[1,2,256,448]{2,3,1,0:T(8,128)(2,1)}, u32[]{:S(2)}) copy-start(bf16[1,2,256,448]{2,3,1,0:T(8,128)(2,1)} %param.11) | copy-start | bytes 1376260
  10.7 209.3 %all-reduce.7.cloned.1.call-start = ((), (), s32[]{:S(2)}) async-start(), calls=%async_computation.1 | async-start | bytes 262144 | tf_op jit(solution)/shard_map/psum | solution.py:30
  149.5 194.5 %all-reduce.9.cloned.1.call-start = ((), (), s32[]{:S(2)}) async-start(), calls=%async_computation.2 | async-start | bytes 131072 | tf_op jit(solution)/shard_map/psum | solution.py:20
  222.3 206.4 %all-reduce.11.cloned.1.call-start = ((), (), s32[]{:S(2)}) async-start(), calls=%async_computation.3 | async-start | bytes 262144 | tf_op jit(solution)/shard_map/psum | solution.py:30
  345.2 11.0 %copy-start.4 = (f32[2,256,32]{1,2,0:T(8,128)S(1)}, f32[2,256,32]{1,2,0:T(8,128)}, u32[]{:S(2)}) copy-start(f32[2,256,32]{1,2,0:T(8,128)} %all-reduce.9.cloned.1.call-done) | copy-start | bytes 196612
  358.1 0.9 copy-start.6
  359.0 0.9 copy-start.7
  428.7 1.9 copy-start.3
  430.6 13.8 %copy-start.10 = (bf16[1,5,448]{2,1,0:T(8,128)(2,1)S(1)}, bf16[1,5,448]{2,1,0:T(8,128)(2,1)}, u32[]{:S(2)}) copy-start(bf16[1,5,448]{2,1,0:T(8,128)(2,1)} %param.16) | copy-start | bytes 13444
  431.5 10.4 %collective-permute-start = (bf16[2,32,448]{1,2,0:T(8,128)(2,1)}, bf16[2,32,448]{1,2,0:T(8,128)(2,1)S(1)}, u32[]{:S(2)}, u32[]{:S(2)}) collective-permute-start(bf16[2,32,448]{1,2,0:T(8,128)(2,1)} %get-tuple-element.19), channel_id=1, source_target_pairs={{0,4},{4,8},{8,12},{12,16},{16,20},{20,24},{24,28},{28,0},{1,5},{5... | collective-permute-start | bytes 172040 | tf_op jit(solution)/shard_map/ppermute | solution.py:47
  432.3 47.4 %collective-permute-start.1 = (bf16[2,32,448]{1,2,0:T(8,128)(2,1)}, bf16[2,32,448]{1,2,0:T(8,128)(2,1)S(1)}, u32[]{:S(2)}, u32[]{:S(2)}) collective-permute-start(bf16[2,32,448]{1,2,0:T(8,128)(2,1)} %get-tuple-element.19), channel_id=1, source_target_pairs={{0,28},{4,0},{8,4},{12,8},{16,12},{20,16},{24,20},{28,24},{1,29},{... | collective-permute-start | bytes 172040 | tf_op jit(solution)/shard_map/ppermute | solution.py:52
  441.9 37.8 %collective-permute-start.2 = (bf16[2,32,448]{1,2,0:T(8,128)(2,1)S(1)}, bf16[2,32,448]{1,2,0:T(8,128)(2,1)}, u32[]{:S(2)}, u32[]{:S(2)}) collective-permute-start(bf16[2,32,448]{1,2,0:T(8,128)(2,1)S(1)} %collective-permute-done), channel_id=1, source_target_pairs={{0,4},{4,8},{8,12},{12,16},{16,20},{20,24},{24,28},{28,0},{1,5},{5... | collective-permute-start | bytes 172040 | tf_op jit(solution)/shard_map/ppermute | solution.py:47
  444.4 37.3 %copy-start.8 = (f32[5,448]{1,0:T(8,128)S(1)}, f32[5,448]{1,0:T(8,128)}, u32[]{:S(2)}) copy-start(f32[5,448]{1,0:T(8,128)} %param.18) | copy-start | bytes 26884
  444.4 37.3 %copy-start.9 = (f32[5,448]{1,0:T(8,128)S(1)}, f32[5,448]{1,0:T(8,128)}, u32[]{:S(2)}) copy-start(f32[5,448]{1,0:T(8,128)} %param.17) | copy-start | bytes 26884
  479.7 9.6 %collective-permute-start.3 = (bf16[2,32,448]{1,2,0:T(8,128)(2,1)S(1)}, bf16[2,32,448]{1,2,0:T(8,128)(2,1)}, u32[]{:S(2)}, u32[]{:S(2)}) collective-permute-start(bf16[2,32,448]{1,2,0:T(8,128)(2,1)S(1)} %collective-permute-done.1), channel_id=1, source_target_pairs={{0,28},{4,0},{8,4},{12,8},{16,12},{20,16},{24,20},{28,24},{1,29},{... | collective-permute-start | bytes 172040 | tf_op jit(solution)/shard_map/ppermute | solution.py:52
  479.7 9.6 %collective-permute-start.4 = (bf16[2,32,448]{1,2,0:T(8,128)(2,1)}, bf16[2,32,448]{1,2,0:T(8,128)(2,1)}, u32[]{:S(2)}, u32[]{:S(2)}) collective-permute-start(bf16[2,32,448]{1,2,0:T(8,128)(2,1)} %collective-permute-done.2), channel_id=1, source_target_pairs={{0,4},{4,8},{8,12},{12,16},{16,20},{20,24},{24,28},{28,0},{1,5},{5... | collective-permute-start | bytes 172040 | tf_op jit(solution)/shard_map/ppermute | solution.py:47
  489.3 16.5 %collective-permute-start.5 = (bf16[2,32,448]{1,2,0:T(8,128)(2,1)}, bf16[2,32,448]{1,2,0:T(8,128)(2,1)}, u32[]{:S(2)}, u32[]{:S(2)}) collective-permute-start(bf16[2,32,448]{1,2,0:T(8,128)(2,1)} %collective-permute-done.3), channel_id=1, source_target_pairs={{0,28},{4,0},{8,4},{12,8},{16,12},{20,16},{24,20},{28,24},{1,29},{... | collective-permute-start | bytes 172040 | tf_op jit(solution)/shard_map/ppermute | solution.py:52
  489.3 19.0 %collective-permute-start.6 = (bf16[2,32,448]{1,2,0:T(8,128)(2,1)}, bf16[2,32,448]{1,2,0:T(8,128)(2,1)}, u32[]{:S(2)}, u32[]{:S(2)}) collective-permute-start(bf16[2,32,448]{1,2,0:T(8,128)(2,1)} %collective-permute-done.4), channel_id=1, source_target_pairs={{0,4},{4,8},{8,12},{12,16},{16,20},{20,24},{24,28},{28,0},{1,5},{5... | collective-permute-start | bytes 172040 | tf_op jit(solution)/shard_map/ppermute | solution.py:47
  510.0 0.8 copy-start.5
Sparse Core Ops, SparseCore 0:
  14.2 120.2 all-reduce.4
  149.6 70.4 all-reduce.6
  227.1 116.7 all-reduce.8
  358.2 70.4 all-reduce.10
